TPU v7x, 32 devices: a whole 2x2x4 slice. The times are simulated.
32 devices in a mesh: clip: 8 (over z, x), row: 4 (over y, core).
Axes of the slice: x: 2, y: 2, z: 4, core: 2. Of those that a mesh axis runs over, the one named last changes fastest.
Arguments:
- features: bfloat16 [8, 128, 32, 256], P('clip', None, 'row'), may hold values from -6 to 6
- out_weight: bfloat16 [3, 128, 3, 3], replicated, may hold values from -0.1875 to 0.1875
- out_bias: float32 [3], replicated, may hold values from -0.5 to 0.5
- targets: bfloat16 [8, 3, 32, 256], P('clip', None, 'row'), may hold values from -1 to 1
- weight_one: bfloat16 [64, 3, 3, 3], replicated, may hold values from -1.25 to 1.25
- bias_one: float32 [64], replicated, may hold values from -0.2 to 0.2
- weight_two: bfloat16 [64, 64, 3, 3], replicated, may hold values from -0.375 to 0.375
- bias_two: float32 [64], replicated, may hold values from -0.2 to 0.2
- weight_three: bfloat16 [128, 64, 3, 3], replicated, may hold values from -0.375 to 0.375
- bias_three: float32 [128], replicated, may hold values from -0.2 to 0.2
- weight_four: bfloat16 [128, 128, 3, 3], replicated, may hold values from -0.25 to 0.25
- bias_four: float32 [128], replicated, may hold values from -0.2 to 0.2
- lin_one: float32 [64], replicated, may hold values from 0.05 to 0.5
- lin_two: float32 [128], replicated, may hold values from 0.05 to 0.5
Outputs:
- loss: float32 [], replicated
- feature_grad: bfloat16 [8, 128, 32, 256], P('clip', None, 'row')
- out_weight_grad: float32 [3, 128, 3, 3], replicated
- out_bias_grad: float32 [3], replicated
All inputs are finite; a program needn't handle non-finite values.
Results may differ from a plain program's by a relative error of at most 0.02.
Values may be sent and summed in bfloat16 or wider, within the bound.
A program may use at most 64 MiB of HBM per device.

v0:
```python
import math
import jax
import jax.numpy as jnp
from jax import lax
from jax.sharding import PartitionSpec as P

shift_values = [-0.03, -0.088, -0.188]
scale_values = [0.458, 0.448, 0.45]


def padded_2(array, sides, width):
    for axis, dim in sides:
        size, length = (lax.axis_size(axis), array.shape[dim])
        up = [(i, (i + 1) % size) for i in range(size - 1)]
        down = [(j, i) for i, j in up]
        last = lax.slice_in_dim(array, length - width, length, axis=dim)
        leading = lax.slice_in_dim(array, 0, width, axis=dim)
        before = lax.ppermute(last, axis, up)
        after = lax.ppermute(leading, axis, down)
        array = jnp.concatenate([before, array, after], axis=dim)
    return array


def shifted(array, axis, by):
    size = lax.axis_size(axis)
    pairs = [(i, i + by) for i in range(size) if 0 <= i + by < size]
    return lax.ppermute(array, axis, pairs)


def shift_array():
    return jnp.array(shift_values, jnp.float32).reshape(1, 3, 1, 1)


def scale_array():
    return jnp.array(scale_values, jnp.float32).reshape(1, 3, 1, 1)


def gelu_exact(values):
    return values * 0.5 * (1.0 + jax.scipy.special.erf(values / math.sqrt(2.0)))


def gelu_slope(values):
    normal_cdf = 0.5 * (1.0 + jax.scipy.special.erf(values / math.sqrt(2.0)))
    density = jnp.exp(-0.5 * values * values) / math.sqrt(2.0 * math.pi)
    return normal_cdf + values * density


def pad_rows(inputs):
    return jnp.pad(inputs, ((0, 0), (0, 0), (1, 1), (0, 0)))


def flipped(weight):
    return jnp.flip(weight, (2, 3)).transpose(1, 0, 2, 3)


def conv_valid(padded, weight):
    frame_count, channels, row_total, col_count = padded.shape
    row_count = row_total - 2
    outputs = weight.shape[0]
    wide = jnp.pad(padded, ((0, 0), (0, 0), (0, 0), (1, 1)))
    total = jnp.zeros((outputs, row_count * col_count), jnp.float32)
    for row_shift in range(3):
        for col_shift in range(3):
            piece = wide[0, :, row_shift : row_shift + row_count, col_shift : col_shift + col_count]
            total = total + jnp.dot(
                weight[:, :, row_shift, col_shift],
                piece.reshape(channels, row_count * col_count),
                preferred_element_type=jnp.float32,
            )
    results = [total.reshape(outputs, row_count, col_count)]
    return jnp.stack(results)


def grad_from_output(inputs, grad_pad):
    frame_count, channels, row_count, col_count = inputs.shape
    outputs = grad_pad.shape[1]
    wide = jnp.pad(grad_pad, ((0, 0), (0, 0), (0, 0), (1, 1)))
    blocks = []
    for row_shift in range(3):
        for col_shift in range(3):
            left = wide[
                0,
                :,
                2 - row_shift : 2 - row_shift + row_count,
                2 - col_shift : 2 - col_shift + col_count,
            ].reshape(outputs, row_count * col_count)
            right = inputs[0].reshape(channels, row_count * col_count)
            total = lax.dot_general(
                left, right, (((1,), (1,)), ((), ())), preferred_element_type=jnp.float32
            )
            blocks.append(total)
    return jnp.stack(blocks).reshape(3, 3, outputs, channels).transpose(2, 3, 0, 1)


def edge_terms(row_values, kernel_row):
    col_count = row_values.shape[2]
    wide = jnp.pad(row_values, ((0, 0), (0, 0), (1, 1)))
    total = jnp.zeros((row_values.shape[0], kernel_row.shape[0], col_count), jnp.float32)
    for col_shift in range(3):
        total = total + jnp.einsum(
            "oc,fcw->fow",
            kernel_row[:, :, col_shift],
            wide[:, :, col_shift : col_shift + col_count],
            preferred_element_type=jnp.float32,
        )
    return total


def pool_mean(values):
    frame_count, channels, row_count, col_count = values.shape
    return values.reshape(frame_count, channels, row_count // 2, 2, col_count // 2, 2).mean(
        axis=(3, 5)
    )


def upsample(values):
    return jnp.repeat(jnp.repeat(values, 2, 2), 2, 3)


def vgg_forward(image, weights):
    weight_one, bias_one, weight_two, bias_two, weight_three, bias_three, weight_four, bias_four = (
        weights
    )
    image_pad = padded_2(image, (("row", 2),), 1)
    pre_one = conv_valid(image_pad, weight_one) + bias_one[None, :, None, None]
    act_one = gelu_exact(pre_one).astype(jnp.bfloat16)
    act_pad = padded_2(act_one, (("row", 2),), 1)
    pre_two = conv_valid(act_pad, weight_two) + bias_two[None, :, None, None]
    act_two = gelu_exact(pre_two)
    pooled = pool_mean(act_two).astype(jnp.bfloat16)
    pooled_pad = padded_2(pooled, (("row", 2),), 1)
    pre_three = conv_valid(pooled_pad, weight_three) + bias_three[None, :, None, None]
    act_three = gelu_exact(pre_three).astype(jnp.bfloat16)
    three_pad = padded_2(act_three, (("row", 2),), 1)
    pre_four = conv_valid(three_pad, weight_four) + bias_four[None, :, None, None]
    act_four = gelu_exact(pre_four)
    return (pre_one, pre_two, act_two, pre_three, pre_four, act_four)


def lpips_layer(feat_dec, feat_tgt, lin, count):
    norm_dec = jnp.sqrt(jnp.sum(feat_dec * feat_dec, 1, keepdims=True) + 1e-06)
    norm_tgt = jnp.sqrt(jnp.sum(feat_tgt * feat_tgt, 1, keepdims=True) + 1e-06)
    unit_dec = feat_dec / norm_dec
    differ = unit_dec - feat_tgt / norm_tgt
    scaled = lin[None, :, None, None]
    part = jnp.sum(scaled * differ * differ) / count
    grad_unit = 2.0 * scaled * differ / count
    grad_feat = (grad_unit - unit_dec * jnp.sum(grad_unit * unit_dec, 1, keepdims=True)) / norm_dec
    return (part, grad_feat)


def local(
    features,
    out_weight,
    out_bias,
    targets,
    weight_one,
    bias_one,
    weight_two,
    bias_two,
    weight_three,
    bias_three,
    weight_four,
    bias_four,
    lin_one,
    lin_two,
):
    weights = (
        weight_one,
        bias_one,
        weight_two,
        bias_two,
        weight_three,
        bias_three,
        weight_four,
        bias_four,
    )
    row_count = features.shape[2]
    width = features.shape[3]
    height = row_count * lax.axis_size("row")
    pre_out = conv_valid(pad_rows(features), out_weight)
    down_terms = edge_terms(features[:, :, row_count - 1, :], out_weight[:, :, 0, :])
    up_terms = edge_terms(features[:, :, 0, :], out_weight[:, :, 2, :])
    from_above = shifted(down_terms, "row", 1)
    from_below = shifted(up_terms, "row", -1)
    pre_out = pre_out.at[:, :, 0, :].add(from_above)
    pre_out = pre_out.at[:, :, row_count - 1, :].add(from_below)
    decoded = (pre_out + out_bias[None, :, None, None]).astype(jnp.bfloat16)
    image_dec = ((decoded.astype(jnp.float32) - shift_array()) / scale_array()).astype(jnp.bfloat16)
    image_tgt = ((targets.astype(jnp.float32) - shift_array()) / scale_array()).astype(jnp.bfloat16)
    pre_one, pre_two, act_two, pre_three, pre_four, act_four = vgg_forward(image_dec, weights)
    tgt_acts = vgg_forward(image_tgt, weights)
    part_one, grad_two = lpips_layer(act_two, tgt_acts[2], lin_one, float(height * width))
    part_two, grad_four = lpips_layer(
        act_four, tgt_acts[5], lin_two, float(height // 2 * (width // 2))
    )
    grad_pre4 = (grad_four * gelu_slope(pre_four)).astype(jnp.bfloat16)
    grad_act3 = conv_valid(padded_2(grad_pre4, (("row", 2),), 1), flipped(weight_four))
    grad_pre3 = (grad_act3 * gelu_slope(pre_three)).astype(jnp.bfloat16)
    grad_pool = conv_valid(padded_2(grad_pre3, (("row", 2),), 1), flipped(weight_three))
    grad_pre2 = ((grad_two + 0.25 * upsample(grad_pool)) * gelu_slope(pre_two)).astype(jnp.bfloat16)
    grad_act1 = conv_valid(padded_2(grad_pre2, (("row", 2),), 1), flipped(weight_two))
    grad_pre1 = (grad_act1 * gelu_slope(pre_one)).astype(jnp.bfloat16)
    grad_image = conv_valid(padded_2(grad_pre1, (("row", 2),), 1), flipped(weight_one))
    grad_dec = (grad_image / scale_array()).astype(jnp.bfloat16)
    grad_pad = padded_2(grad_dec, (("row", 2),), 1)
    feature_grad = conv_valid(grad_pad, flipped(out_weight)).astype(jnp.bfloat16)
    weight_grad = grad_from_output(features, grad_pad)
    bias_grad = jnp.sum(grad_dec.astype(jnp.float32), (0, 2, 3))
    loss, weight_total, bias_total = lax.psum(
        (part_one + part_two, weight_grad, bias_grad), ("clip", "row")
    )
    return (loss, feature_grad, weight_total, bias_total)


def solution(mesh):
    placed = (
        P("clip", None, "row", None),
        P(),
        P(),
        P("clip", None, "row", None),
        P(),
        P(),
        P(),
        P(),
        P(),
        P(),
        P(),
        P(),
        P(),
        P(),
    )
    return jax.shard_map(
        local,
        mesh=mesh,
        in_specs=placed,
        out_specs=(P(), P("clip", None, "row", None), P(), P()),
        check_vma=False,
    )
```

profile of v0, /device:TPU:0, one launch (start us, length us, event | category | flops | bytes accessed | tf_op | source)
XLA Modules:
  0.0 208.2 jit_solution(6531382458531928736)
XLA Ops:
  3.4 2.4 %collective-permute-start = (f32[1,3,256]{2,1,0:T(4,128)S(1)}, f32[1,3,256]{2,1,0:T(4,128)S(1)}, u32[]{:S(2)}, u32[]{:S(2)}) collective-permute-start(f32[1,3,256]{2,1,0:T(4,128)S(1)} %fusion.18), channel_id=1, source_target_pairs={{0,1},{1,2},{2,3},{4,5},{5,6},{6,7},{8,9},{9,10},{10,11},{12,13},{... | collective-permute-start | bytes 9224 | tf_op jit(solution)/shard_map/ppermute | solution.py:27
  15.8 5.2 %collective-permute-start.2 = (bf16[1,3,1,256]{3,1,2,0:T(4,128)(2,1)S(1)}, bf16[1,3,1,256]{3,1,2,0:T(4,128)(2,1)S(1)}, u32[]{:S(2)}, u32[]{:S(2)}) collective-permute-start(bf16[1,3,1,256]{3,1,2,0:T(4,128)(2,1)S(1)} %get-tuple-element.202), channel_id=1, source_target_pairs={{0,1},{1,2},{2,3},{4,5},{5,6},{6,7},{8,9},{9,10},{10,11},{12,13},{... | collective-permute-start | bytes 4616 | tf_op jit(solution)/shard_map/ppermute | solution.py:18
  22.2 4.3 %collective-permute-start.6 = (bf16[1,3,1,256]{3,1,2,0:T(4,128)(2,1)S(1)}, bf16[1,3,1,256]{3,1,2,0:T(4,128)(2,1)S(1)}, u32[]{:S(2)}, u32[]{:S(2)}) collective-permute-start(bf16[1,3,1,256]{3,1,2,0:T(4,128)(2,1)S(1)} %get-tuple-element.198), channel_id=1, source_target_pairs={{0,1},{1,2},{2,3},{4,5},{5,6},{6,7},{8,9},{9,10},{10,11},{12,13},{... | collective-permute-start | bytes 4616 | tf_op jit(solution)/shard_map/ppermute | solution.py:18
  34.3 4.3 %collective-permute-start.8 = (bf16[1,64,1,256]{3,2,1,0:T(2,128)(2,1)S(1)}, bf16[1,64,1,256]{3,2,1,0:T(2,128)(2,1)S(1)}, u32[]{:S(2)}, u32[]{:S(2)}) collective-permute-start(bf16[1,64,1,256]{3,2,1,0:T(2,128)(2,1)S(1)} %get-tuple-element.108), channel_id=1, source_target_pairs={{0,1},{1,2},{2,3},{4,5},{5,6},{6,7},{8,9},{9,10},{10,11},{12,13},{... | collective-permute-start | bytes 98312 | tf_op jit(solution)/shard_map/ppermute | solution.py:18
  40.1 4.2 %collective-permute-start.4 = (bf16[1,64,1,256]{3,2,1,0:T(2,128)(2,1)S(1)}, bf16[1,64,1,256]{3,2,1,0:T(2,128)(2,1)S(1)}, u32[]{:S(2)}, u32[]{:S(2)}) collective-permute-start(bf16[1,64,1,256]{3,2,1,0:T(2,128)(2,1)S(1)} %get-tuple-element.112), channel_id=1, source_target_pairs={{0,1},{1,2},{2,3},{4,5},{5,6},{6,7},{8,9},{9,10},{10,11},{12,13},{... | collective-permute-start | bytes 98312 | tf_op jit(solution)/shard_map/ppermute | solution.py:18
  46.1 2.5 %collective-permute-done.5 = bf16[1,64,1,256]{3,2,1,0:T(2,128)(2,1)S(1)} collective-permute-done((bf16[1,64,1,256]{3,2,1,0:T(2,128)(2,1)S(1)}, bf16[1,64,1,256]{3,2,1,0:T(2,128)(2,1)S(1)}, u32[]{:S(2)}, u32[]{:S(2)}) %collective-permute-start.5) | collective-permute-done | bytes 32800 | tf_op jit(solution)/shard_map/ppermute | solution.py:19
  60.3 2.1 %copy.253 = f32[1,64,4,2,128,2]{4,1,5,3,2,0:T(8,128)} copy(f32[1,64,4,2,128,2]{1,5,4,3,2,0:T(2,128)} %bitcast.1069) | data formatting | bytes 1048576 | tf_op jit(solution)/shard_map/stack;reshape | solution.py:71
  62.5 2.1 multiply_reduce_fusion.2
  66.5 4.8 %collective-permute-start.14 = (bf16[1,64,1,128]{1,3,2,0:T(8,128)(2,1)S(1)}, bf16[1,64,1,128]{1,3,2,0:T(8,128)(2,1)S(1)}, u32[]{:S(2)}, u32[]{:S(2)}) collective-permute-start(bf16[1,64,1,128]{1,3,2,0:T(8,128)(2,1)S(1)} %get-tuple-element.172), channel_id=1, source_target_pairs={{0,1},{1,2},{2,3},{4,5},{5,6},{6,7},{8,9},{9,10},{10,11},{12,13},{... | collective-permute-start | bytes 49160 | tf_op jit(solution)/shard_map/ppermute | solution.py:18
  72.8 3.0 %collective-permute-start.10 = (bf16[1,64,1,128]{1,3,2,0:T(8,128)(2,1)S(1)}, bf16[1,64,1,128]{1,3,2,0:T(8,128)(2,1)S(1)}, u32[]{:S(2)}, u32[]{:S(2)}) collective-permute-start(bf16[1,64,1,128]{1,3,2,0:T(8,128)(2,1)S(1)} %get-tuple-element.164), channel_id=1, source_target_pairs={{0,1},{1,2},{2,3},{4,5},{5,6},{6,7},{8,9},{9,10},{10,11},{12,13},{... | collective-permute-start | bytes 49160 | tf_op jit(solution)/shard_map/ppermute | solution.py:18
  77.8 2.0 collective-permute-done.11
  83.6 4.5 %collective-permute-start.16 = (bf16[1,128,1,128]{1,3,2,0:T(8,128)(2,1)S(1)}, bf16[1,128,1,128]{1,3,2,0:T(8,128)(2,1)S(1)}, u32[]{:S(2)}, u32[]{:S(2)}) collective-permute-start(bf16[1,128,1,128]{1,3,2,0:T(8,128)(2,1)S(1)} %get-tuple-element.168), channel_id=1, source_target_pairs={{0,1},{1,2},{2,3},{4,5},{5,6},{6,7},{8,9},{9,10},{10,11},{12,13},{... | collective-permute-start | bytes 98312 | tf_op jit(solution)/shard_map/ppermute | solution.py:18
  89.5 3.0 %collective-permute-start.12 = (bf16[1,128,1,128]{1,3,2,0:T(8,128)(2,1)S(1)}, bf16[1,128,1,128]{1,3,2,0:T(8,128)(2,1)S(1)}, u32[]{:S(2)}, u32[]{:S(2)}) collective-permute-start(bf16[1,128,1,128]{1,3,2,0:T(8,128)(2,1)S(1)} %get-tuple-element.160), channel_id=1, source_target_pairs={{0,1},{1,2},{2,3},{4,5},{5,6},{6,7},{8,9},{9,10},{10,11},{12,13},{... | collective-permute-start | bytes 98312 | tf_op jit(solution)/shard_map/ppermute | solution.py:18
  100.4 4.7 %collective-permute-start.18 = (bf16[1,128,1,128]{1,3,2,0:T(8,128)(2,1)S(1)}, bf16[1,128,1,128]{1,3,2,0:T(8,128)(2,1)S(1)}, u32[]{:S(2)}, u32[]{:S(2)}) collective-permute-start(bf16[1,128,1,128]{1,3,2,0:T(8,128)(2,1)S(1)} %get-tuple-element.156), channel_id=1, source_target_pairs={{0,1},{1,2},{2,3},{4,5},{5,6},{6,7},{8,9},{9,10},{10,11},{12,13},{... | collective-permute-start | bytes 98312 | tf_op jit(solution)/shard_map/ppermute | solution.py:18
  106.4 1.8 collective-permute-done.19
  110.4 4.1 %collective-permute-start.20 = (bf16[1,128,1,128]{1,3,2,0:T(8,128)(2,1)S(1)}, bf16[1,128,1,128]{1,3,2,0:T(8,128)(2,1)S(1)}, u32[]{:S(2)}, u32[]{:S(2)}) collective-permute-start(bf16[1,128,1,128]{1,3,2,0:T(8,128)(2,1)S(1)} %get-tuple-element.152), channel_id=1, source_target_pairs={{0,1},{1,2},{2,3},{4,5},{5,6},{6,7},{8,9},{9,10},{10,11},{12,13},{... | collective-permute-start | bytes 98312 | tf_op jit(solution)/shard_map/ppermute | solution.py:18
  116.1 1.7 multiply_reduce_fusion
  124.0 2.0 fusion.35
  126.7 3.6 %collective-permute-start.22 = (bf16[1,64,1,256]{3,2,1,0:T(2,128)(2,1)}, bf16[1,64,1,256]{3,2,1,0:T(2,128)(2,1)}, u32[]{:S(2)}, u32[]{:S(2)}) collective-permute-start(bf16[1,64,1,256]{3,2,1,0:T(2,128)(2,1)} %get-tuple-element.104), channel_id=1, source_target_pairs={{0,1},{1,2},{2,3},{4,5},{5,6},{6,7},{8,9},{9,10},{10,11},{12,13},{... | collective-permute-start | bytes 98312 | tf_op jit(solution)/shard_map/ppermute | solution.py:18
  141.2 3.3 %collective-permute-start.24 = (bf16[1,64,1,256]{3,2,1,0:T(2,128)(2,1)S(1)}, bf16[1,64,1,256]{3,2,1,0:T(2,128)(2,1)S(1)}, u32[]{:S(2)}, u32[]{:S(2)}) collective-permute-start(bf16[1,64,1,256]{3,2,1,0:T(2,128)(2,1)S(1)} %get-tuple-element.100), channel_id=1, source_target_pairs={{0,1},{1,2},{2,3},{4,5},{5,6},{6,7},{8,9},{9,10},{10,11},{12,13},{... | collective-permute-start | bytes 98312 | tf_op jit(solution)/shard_map/ppermute | solution.py:18
  146.0 2.8 %collective-permute-done.25 = bf16[1,64,1,256]{3,2,1,0:T(2,128)(2,1)S(1)} collective-permute-done((bf16[1,64,1,256]{3,2,1,0:T(2,128)(2,1)S(1)}, bf16[1,64,1,256]{3,2,1,0:T(2,128)(2,1)S(1)}, u32[]{:S(2)}, u32[]{:S(2)}) %collective-permute-start.25) | collective-permute-done | bytes 32800 | tf_op jit(solution)/shard_map/ppermute | solution.py:19
  151.5 4.8 %collective-permute-start.26 = (bf16[1,3,1,256]{3,1,2,0:T(4,128)(2,1)S(1)}, bf16[1,3,1,256]{3,1,2,0:T(4,128)(2,1)S(1)}, u32[]{:S(2)}, u32[]{:S(2)}) collective-permute-start(bf16[1,3,1,256]{3,1,2,0:T(4,128)(2,1)S(1)} %get-tuple-element.194), channel_id=1, source_target_pairs={{0,1},{1,2},{2,3},{4,5},{5,6},{6,7},{8,9},{9,10},{10,11},{12,13},{... | collective-permute-start | bytes 4616 | tf_op jit(solution)/shard_map/ppermute | solution.py:18
  156.4 1.6 collective-permute-start.27
  166.7 41.5 %all-reduce.17 = (f32[]{:T(128)}, f32[3,128,3,3]{1,3,2,0:T(4,128)}, f32[3]{0:T(128)}) all-reduce(f32[]{:T(128)S(6)} %add.1136, f32[3,128,3,3]{1,3,2,0:T(4,128)S(1)} %bitcast.1222, f32[3]{0:T(128)S(1)} %get-tuple-element.57), channel_id=1, replica_groups=mesh['clip'=8,'row'=4] {'clip','row'}, use_global_device_ids=true, to_apply=%region_8.9 | all-reduce | flops 3460 | bytes 27680 | tf_op jit(solution)/shard_map/psum | solution.py:210
  (418 shorter events, 87.7 us)
Async XLA Ops:
  3.4 12.2 %collective-permute-start = (f32[1,3,256]{2,1,0:T(4,128)S(1)}, f32[1,3,256]{2,1,0:T(4,128)S(1)}, u32[]{:S(2)}, u32[]{:S(2)}) collective-permute-start(f32[1,3,256]{2,1,0:T(4,128)S(1)} %fusion.18), channel_id=1, source_target_pairs={{0,1},{1,2},{2,3},{4,5},{5,6},{6,7},{8,9},{9,10},{10,11},{12,13},{... | collective-permute-start | bytes 9224 | tf_op jit(solution)/shard_map/ppermute | solution.py:27
  6.4 9.2 %collective-permute-start.1 = (f32[1,3,256]{2,1,0:T(4,128)S(1)}, f32[1,3,256]{2,1,0:T(4,128)S(1)}, u32[]{:S(2)}, u32[]{:S(2)}) collective-permute-start(f32[1,3,256]{2,1,0:T(4,128)S(1)} %fusion.17), channel_id=1, source_target_pairs={{1,0},{2,1},{3,2},{5,4},{6,5},{7,6},{9,8},{10,9},{11,10},{13,12},{... | collective-permute-start | bytes 9224 | tf_op jit(solution)/shard_map/ppermute | solution.py:27
  15.8 12.1 %collective-permute-start.2 = (bf16[1,3,1,256]{3,1,2,0:T(4,128)(2,1)S(1)}, bf16[1,3,1,256]{3,1,2,0:T(4,128)(2,1)S(1)}, u32[]{:S(2)}, u32[]{:S(2)}) collective-permute-start(bf16[1,3,1,256]{3,1,2,0:T(4,128)(2,1)S(1)} %get-tuple-element.202), channel_id=1, source_target_pairs={{0,1},{1,2},{2,3},{4,5},{5,6},{6,7},{8,9},{9,10},{10,11},{12,13},{... | collective-permute-start | bytes 4616 | tf_op jit(solution)/shard_map/ppermute | solution.py:18
  20.9 6.9 %collective-permute-start.3 = (bf16[1,3,1,256]{3,1,2,0:T(4,128)(2,1)S(1)}, bf16[1,3,1,256]{3,1,2,0:T(4,128)(2,1)S(1)}, u32[]{:S(2)}, u32[]{:S(2)}) collective-permute-start(bf16[1,3,1,256]{3,1,2,0:T(4,128)(2,1)S(1)} %get-tuple-element.203), channel_id=1, source_target_pairs={{1,0},{2,1},{3,2},{5,4},{6,5},{7,6},{9,8},{10,9},{11,10},{13,12},{... | collective-permute-start | bytes 4616 | tf_op jit(solution)/shard_map/ppermute | solution.py:19
  22.2 8.5 %collective-permute-start.6 = (bf16[1,3,1,256]{3,1,2,0:T(4,128)(2,1)S(1)}, bf16[1,3,1,256]{3,1,2,0:T(4,128)(2,1)S(1)}, u32[]{:S(2)}, u32[]{:S(2)}) collective-permute-start(bf16[1,3,1,256]{3,1,2,0:T(4,128)(2,1)S(1)} %get-tuple-element.198), channel_id=1, source_target_pairs={{0,1},{1,2},{2,3},{4,5},{5,6},{6,7},{8,9},{9,10},{10,11},{12,13},{... | collective-permute-start | bytes 4616 | tf_op jit(solution)/shard_map/ppermute | solution.py:18
  26.5 4.3 %collective-permute-start.7 = (bf16[1,3,1,256]{3,1,2,0:T(4,128)(2,1)S(1)}, bf16[1,3,1,256]{3,1,2,0:T(4,128)(2,1)S(1)}, u32[]{:S(2)}, u32[]{:S(2)}) collective-permute-start(bf16[1,3,1,256]{3,1,2,0:T(4,128)(2,1)S(1)} %get-tuple-element.199), channel_id=1, source_target_pairs={{1,0},{2,1},{3,2},{5,4},{6,5},{7,6},{9,8},{10,9},{11,10},{13,12},{... | collective-permute-start | bytes 4616 | tf_op jit(solution)/shard_map/ppermute | solution.py:19
  34.3 11.5 %collective-permute-start.8 = (bf16[1,64,1,256]{3,2,1,0:T(2,128)(2,1)S(1)}, bf16[1,64,1,256]{3,2,1,0:T(2,128)(2,1)S(1)}, u32[]{:S(2)}, u32[]{:S(2)}) collective-permute-start(bf16[1,64,1,256]{3,2,1,0:T(2,128)(2,1)S(1)} %get-tuple-element.108), channel_id=1, source_target_pairs={{0,1},{1,2},{2,3},{4,5},{5,6},{6,7},{8,9},{9,10},{10,11},{12,13},{... | collective-permute-start | bytes 98312 | tf_op jit(solution)/shard_map/ppermute | solution.py:18
  38.5 7.2 %collective-permute-start.9 = (bf16[1,64,1,256]{3,2,1,0:T(2,128)(2,1)S(1)}, bf16[1,64,1,256]{3,2,1,0:T(2,128)(2,1)S(1)}, u32[]{:S(2)}, u32[]{:S(2)}) collective-permute-start(bf16[1,64,1,256]{3,2,1,0:T(2,128)(2,1)S(1)} %get-tuple-element.109), channel_id=1, source_target_pairs={{1,0},{2,1},{3,2},{5,4},{6,5},{7,6},{9,8},{10,9},{11,10},{13,12},{... | collective-permute-start | bytes 98312 | tf_op jit(solution)/shard_map/ppermute | solution.py:19
  40.1 6.1 %collective-permute-start.4 = (bf16[1,64,1,256]{3,2,1,0:T(2,128)(2,1)S(1)}, bf16[1,64,1,256]{3,2,1,0:T(2,128)(2,1)S(1)}, u32[]{:S(2)}, u32[]{:S(2)}) collective-permute-start(bf16[1,64,1,256]{3,2,1,0:T(2,128)(2,1)S(1)} %get-tuple-element.112), channel_id=1, source_target_pairs={{0,1},{1,2},{2,3},{4,5},{5,6},{6,7},{8,9},{9,10},{10,11},{12,13},{... | collective-permute-start | bytes 98312 | tf_op jit(solution)/shard_map/ppermute | solution.py:18
  44.3 4.4 %collective-permute-start.5 = (bf16[1,64,1,256]{3,2,1,0:T(2,128)(2,1)S(1)}, bf16[1,64,1,256]{3,2,1,0:T(2,128)(2,1)S(1)}, u32[]{:S(2)}, u32[]{:S(2)}) collective-permute-start(bf16[1,64,1,256]{3,2,1,0:T(2,128)(2,1)S(1)} %get-tuple-element.113), channel_id=1, source_target_pairs={{1,0},{2,1},{3,2},{5,4},{6,5},{7,6},{9,8},{10,9},{11,10},{13,12},{... | collective-permute-start | bytes 98312 | tf_op jit(solution)/shard_map/ppermute | solution.py:19
  66.5 10.7 %collective-permute-start.14 = (bf16[1,64,1,128]{1,3,2,0:T(8,128)(2,1)S(1)}, bf16[1,64,1,128]{1,3,2,0:T(8,128)(2,1)S(1)}, u32[]{:S(2)}, u32[]{:S(2)}) collective-permute-start(bf16[1,64,1,128]{1,3,2,0:T(8,128)(2,1)S(1)} %get-tuple-element.172), channel_id=1, source_target_pairs={{0,1},{1,2},{2,3},{4,5},{5,6},{6,7},{8,9},{9,10},{10,11},{12,13},{... | collective-permute-start | bytes 49160 | tf_op jit(solution)/shard_map/ppermute | solution.py:18
  71.4 5.8 %collective-permute-start.15 = (bf16[1,64,1,128]{1,3,2,0:T(8,128)(2,1)S(1)}, bf16[1,64,1,128]{1,3,2,0:T(8,128)(2,1)S(1)}, u32[]{:S(2)}, u32[]{:S(2)}) collective-permute-start(bf16[1,64,1,128]{1,3,2,0:T(8,128)(2,1)S(1)} %get-tuple-element.173), channel_id=1, source_target_pairs={{1,0},{2,1},{3,2},{5,4},{6,5},{7,6},{9,8},{10,9},{11,10},{13,12},{... | collective-permute-start | bytes 49160 | tf_op jit(solution)/shard_map/ppermute | solution.py:19
  72.8 4.9 %collective-permute-start.10 = (bf16[1,64,1,128]{1,3,2,0:T(8,128)(2,1)S(1)}, bf16[1,64,1,128]{1,3,2,0:T(8,128)(2,1)S(1)}, u32[]{:S(2)}, u32[]{:S(2)}) collective-permute-start(bf16[1,64,1,128]{1,3,2,0:T(8,128)(2,1)S(1)} %get-tuple-element.164), channel_id=1, source_target_pairs={{0,1},{1,2},{2,3},{4,5},{5,6},{6,7},{8,9},{9,10},{10,11},{12,13},{... | collective-permute-start | bytes 49160 | tf_op jit(solution)/shard_map/ppermute | solution.py:18
  83.6 10.2 %collective-permute-start.16 = (bf16[1,128,1,128]{1,3,2,0:T(8,128)(2,1)S(1)}, bf16[1,128,1,128]{1,3,2,0:T(8,128)(2,1)S(1)}, u32[]{:S(2)}, u32[]{:S(2)}) collective-permute-start(bf16[1,128,1,128]{1,3,2,0:T(8,128)(2,1)S(1)} %get-tuple-element.168), channel_id=1, source_target_pairs={{0,1},{1,2},{2,3},{4,5},{5,6},{6,7},{8,9},{9,10},{10,11},{12,13},{... | collective-permute-start | bytes 98312 | tf_op jit(solution)/shard_map/ppermute | solution.py:18
  88.1 5.7 %collective-permute-start.17 = (bf16[1,128,1,128]{1,3,2,0:T(8,128)(2,1)S(1)}, bf16[1,128,1,128]{1,3,2,0:T(8,128)(2,1)S(1)}, u32[]{:S(2)}, u32[]{:S(2)}) collective-permute-start(bf16[1,128,1,128]{1,3,2,0:T(8,128)(2,1)S(1)} %get-tuple-element.169), channel_id=1, source_target_pairs={{1,0},{2,1},{3,2},{5,4},{6,5},{7,6},{9,8},{10,9},{11,10},{13,12},{... | collective-permute-start | bytes 98312 | tf_op jit(solution)/shard_map/ppermute | solution.py:19
  89.5 5.7 %collective-permute-start.12 = (bf16[1,128,1,128]{1,3,2,0:T(8,128)(2,1)S(1)}, bf16[1,128,1,128]{1,3,2,0:T(8,128)(2,1)S(1)}, u32[]{:S(2)}, u32[]{:S(2)}) collective-permute-start(bf16[1,128,1,128]{1,3,2,0:T(8,128)(2,1)S(1)} %get-tuple-element.160), channel_id=1, source_target_pairs={{0,1},{1,2},{2,3},{4,5},{5,6},{6,7},{8,9},{9,10},{10,11},{12,13},{... | collective-permute-start | bytes 98312 | tf_op jit(solution)/shard_map/ppermute | solution.py:18
  100.4 6.0 %collective-permute-start.18 = (bf16[1,128,1,128]{1,3,2,0:T(8,128)(2,1)S(1)}, bf16[1,128,1,128]{1,3,2,0:T(8,128)(2,1)S(1)}, u32[]{:S(2)}, u32[]{:S(2)}) collective-permute-start(bf16[1,128,1,128]{1,3,2,0:T(8,128)(2,1)S(1)} %get-tuple-element.156), channel_id=1, source_target_pairs={{0,1},{1,2},{2,3},{4,5},{5,6},{6,7},{8,9},{9,10},{10,11},{12,13},{... | collective-permute-start | bytes 98312 | tf_op jit(solution)/shard_map/ppermute | solution.py:18
  110.4 9.3 %collective-permute-start.20 = (bf16[1,128,1,128]{1,3,2,0:T(8,128)(2,1)S(1)}, bf16[1,128,1,128]{1,3,2,0:T(8,128)(2,1)S(1)}, u32[]{:S(2)}, u32[]{:S(2)}) collective-permute-start(bf16[1,128,1,128]{1,3,2,0:T(8,128)(2,1)S(1)} %get-tuple-element.152), channel_id=1, source_target_pairs={{0,1},{1,2},{2,3},{4,5},{5,6},{6,7},{8,9},{9,10},{10,11},{12,13},{... | collective-permute-start | bytes 98312 | tf_op jit(solution)/shard_map/ppermute | solution.py:18
  114.5 5.2 %collective-permute-start.21 = (bf16[1,128,1,128]{1,3,2,0:T(8,128)(2,1)S(1)}, bf16[1,128,1,128]{1,3,2,0:T(8,128)(2,1)S(1)}, u32[]{:S(2)}, u32[]{:S(2)}) collective-permute-start(bf16[1,128,1,128]{1,3,2,0:T(8,128)(2,1)S(1)} %get-tuple-element.153), channel_id=1, source_target_pairs={{1,0},{2,1},{3,2},{5,4},{6,5},{7,6},{9,8},{10,9},{11,10},{13,12},{... | collective-permute-start | bytes 98312 | tf_op jit(solution)/shard_map/ppermute | solution.py:19
  126.7 7.8 %collective-permute-start.22 = (bf16[1,64,1,256]{3,2,1,0:T(2,128)(2,1)}, bf16[1,64,1,256]{3,2,1,0:T(2,128)(2,1)}, u32[]{:S(2)}, u32[]{:S(2)}) collective-permute-start(bf16[1,64,1,256]{3,2,1,0:T(2,128)(2,1)} %get-tuple-element.104), channel_id=1, source_target_pairs={{0,1},{1,2},{2,3},{4,5},{5,6},{6,7},{8,9},{9,10},{10,11},{12,13},{... | collective-permute-start | bytes 98312 | tf_op jit(solution)/shard_map/ppermute | solution.py:18
  130.4 5.0 %collective-permute-start.23 = (bf16[1,64,1,256]{3,2,1,0:T(2,128)(2,1)}, bf16[1,64,1,256]{3,2,1,0:T(2,128)(2,1)S(1)}, u32[]{:S(2)}, u32[]{:S(2)}) collective-permute-start(bf16[1,64,1,256]{3,2,1,0:T(2,128)(2,1)} %get-tuple-element.105), channel_id=1, source_target_pairs={{1,0},{2,1},{3,2},{5,4},{6,5},{7,6},{9,8},{10,9},{11,10},{13,12},{... | collective-permute-start | bytes 98312 | tf_op jit(solution)/shard_map/ppermute | solution.py:19
  141.2 4.8 %collective-permute-start.24 = (bf16[1,64,1,256]{3,2,1,0:T(2,128)(2,1)S(1)}, bf16[1,64,1,256]{3,2,1,0:T(2,128)(2,1)S(1)}, u32[]{:S(2)}, u32[]{:S(2)}) collective-permute-start(bf16[1,64,1,256]{3,2,1,0:T(2,128)(2,1)S(1)} %get-tuple-element.100), channel_id=1, source_target_pairs={{0,1},{1,2},{2,3},{4,5},{5,6},{6,7},{8,9},{9,10},{10,11},{12,13},{... | collective-permute-start | bytes 98312 | tf_op jit(solution)/shard_map/ppermute | solution.py:18
  144.5 4.2 %collective-permute-start.25 = (bf16[1,64,1,256]{3,2,1,0:T(2,128)(2,1)S(1)}, bf16[1,64,1,256]{3,2,1,0:T(2,128)(2,1)S(1)}, u32[]{:S(2)}, u32[]{:S(2)}) collective-permute-start(bf16[1,64,1,256]{3,2,1,0:T(2,128)(2,1)S(1)} %get-tuple-element.101), channel_id=1, source_target_pairs={{1,0},{2,1},{3,2},{5,4},{6,5},{7,6},{9,8},{10,9},{11,10},{13,12},{... | collective-permute-start | bytes 98312 | tf_op jit(solution)/shard_map/ppermute | solution.py:19
  151.5 7.7 %collective-permute-start.26 = (bf16[1,3,1,256]{3,1,2,0:T(4,128)(2,1)S(1)}, bf16[1,3,1,256]{3,1,2,0:T(4,128)(2,1)S(1)}, u32[]{:S(2)}, u32[]{:S(2)}) collective-permute-start(bf16[1,3,1,256]{3,1,2,0:T(4,128)(2,1)S(1)} %get-tuple-element.194), channel_id=1, source_target_pairs={{0,1},{1,2},{2,3},{4,5},{5,6},{6,7},{8,9},{9,10},{10,11},{12,13},{... | collective-permute-start | bytes 4616 | tf_op jit(solution)/shard_map/ppermute | solution.py:18
  (43 other events, 118.7 us)
where the time goes:
time: 210 us; the launch traced here: 208 us
  starting transfers between devices  75.1 us (36%)
  blocking collectives  41.5 us (20%)
  matrix products  32.7 us (16%)
  local copies, waits for them, and re-layouts  32.1 us (15%)
  other arithmetic  11.8 us (6%)
  waiting for transfers between devices  10.5 us (5%)
  between operations  4.34 us (2%)
    ppermute x13, starting transfers between devices, padded_2(): before = lax.ppermute(last, axis, up)  53.9 us
    psum x1, blocking collectives, local(): lax.psum((part_one + part_two, weight_grad, bias_grad), ('clip', 'row'))  41.5 us
    dot_general x126, matrix products, conv_valid(): jnp.dot(weight[:, :, row_shift, col_shift], piece.reshape(channels, row_c...  29.1 us
    ppermute x13, starting transfers between devices, padded_2(): after = lax.ppermute(leading, axis, down)  17.6 us
    unnamed x129, local copies, waits for them, and re-layouts  11.2 us
    ppermute x13, waiting for transfers between devices, padded_2(): after = lax.ppermute(leading, axis, down)  10.5 us
  transfers between devices with their start and end apart: 28, of which 7 were waited for; matrix products, arithmetic and copies ran while one was open for 10% of the time, Pallas kernels for 0%

commit v1 on v0

--- a/solution.py
+++ b/solution.py
@@ -208,7 +208,7 @@
     weight_grad = grad_from_output(features, grad_pad)
     bias_grad = jnp.sum(grad_dec.astype(jnp.float32), (0, 2, 3))
     loss, weight_total, bias_total = lax.psum(
-        (part_one + part_two, weight_grad, bias_grad), ("clip", "row")
+        lax.psum((part_one + part_two, weight_grad, bias_grad), "clip"), "row"
     )
     return (loss, feature_grad, weight_total, bias_total)
 

time: 210 us -> 217 us (1.033)
  blocking collectives: 41.5 us -> 49.2 us
    psum x1 -> x2, blocking collectives: 41.5 us -> 49.2 us  [the longest x1 37.9 us: local(): lax.psum((part_one + part_two, weight_grad, bias_grad), 'clip')]
  transfers between devices with their start and end apart: 28 -> 28, of which waited for: 7 -> 7; matrix products, arithmetic and copies ran while one was open for 10% -> 9% of each run, Pallas kernels for 0% -> 0%
where the time goes in v1:
time: 217 us; the launch traced here: 216 us
  starting transfers between devices  75.1 us (35%)
  blocking collectives  49.2 us (23%)
  matrix products  32.8 us (15%)
  local copies, waits for them, and re-layouts  32.1 us (15%)
  other arithmetic  11.9 us (5%)
  waiting for transfers between devices  10.5 us (5%)
  between operations  4.42 us (2%)
    ppermute x13, starting transfers between devices, padded_2(): before = lax.ppermute(last, axis, up)  53.9 us
    psum x1, blocking collectives, local(): lax.psum((part_one + part_two, weight_grad, bias_grad), 'clip')  37.9 us
    dot_general x126, matrix products, conv_valid(): jnp.dot(weight[:, :, row_shift, col_shift], piece.reshape(channels, row_c...  29.1 us
    ppermute x13, starting transfers between devices, padded_2(): after = lax.ppermute(leading, axis, down)  17.6 us
    psum x1, blocking collectives, local(): lax.psum(lax.psum((part_one + part_two, weight_grad, bias_grad), 'clip'),...  11.3 us
    unnamed x129, local copies, waits for them, and re-layouts  11.2 us
    ppermute x13, waiting for transfers between devices, padded_2(): after = lax.ppermute(leading, axis, down)  10.4 us
  transfers between devices with their start and end apart: 28, of which 7 were waited for; matrix products, arithmetic and copies ran while one was open for 9% of the time, Pallas kernels for 0%

profile of v1, /device:TPU:0, one launch (start us, length us, event | category | flops | bytes accessed | tf_op | source)
XLA Modules:
  0.0 216.0 jit_solution(4669753925820176209)
XLA Ops:
  3.4 2.4 %collective-permute-start = (f32[1,3,256]{2,1,0:T(4,128)S(1)}, f32[1,3,256]{2,1,0:T(4,128)S(1)}, u32[]{:S(2)}, u32[]{:S(2)}) collective-permute-start(f32[1,3,256]{2,1,0:T(4,128)S(1)} %fusion.18), channel_id=1, source_target_pairs={{0,1},{1,2},{2,3},{4,5},{5,6},{6,7},{8,9},{9,10},{10,11},{12,13},{... | collective-permute-start | bytes 9224 | tf_op jit(solution)/shard_map/ppermute | solution.py:27
  15.7 5.2 %collective-permute-start.2 = (bf16[1,3,1,256]{3,1,2,0:T(4,128)(2,1)S(1)}, bf16[1,3,1,256]{3,1,2,0:T(4,128)(2,1)S(1)}, u32[]{:S(2)}, u32[]{:S(2)}) collective-permute-start(bf16[1,3,1,256]{3,1,2,0:T(4,128)(2,1)S(1)} %get-tuple-element.205), channel_id=1, source_target_pairs={{0,1},{1,2},{2,3},{4,5},{5,6},{6,7},{8,9},{9,10},{10,11},{12,13},{... | collective-permute-start | bytes 4616 | tf_op jit(solution)/shard_map/ppermute | solution.py:18
  22.2 4.3 %collective-permute-start.6 = (bf16[1,3,1,256]{3,1,2,0:T(4,128)(2,1)S(1)}, bf16[1,3,1,256]{3,1,2,0:T(4,128)(2,1)S(1)}, u32[]{:S(2)}, u32[]{:S(2)}) collective-permute-start(bf16[1,3,1,256]{3,1,2,0:T(4,128)(2,1)S(1)} %get-tuple-element.201), channel_id=1, source_target_pairs={{0,1},{1,2},{2,3},{4,5},{5,6},{6,7},{8,9},{9,10},{10,11},{12,13},{... | collective-permute-start | bytes 4616 | tf_op jit(solution)/shard_map/ppermute | solution.py:18
  34.2 4.3 %collective-permute-start.8 = (bf16[1,64,1,256]{3,2,1,0:T(2,128)(2,1)S(1)}, bf16[1,64,1,256]{3,2,1,0:T(2,128)(2,1)S(1)}, u32[]{:S(2)}, u32[]{:S(2)}) collective-permute-start(bf16[1,64,1,256]{3,2,1,0:T(2,128)(2,1)S(1)} %get-tuple-element.111), channel_id=1, source_target_pairs={{0,1},{1,2},{2,3},{4,5},{5,6},{6,7},{8,9},{9,10},{10,11},{12,13},{... | collective-permute-start | bytes 98312 | tf_op jit(solution)/shard_map/ppermute | solution.py:18
  40.0 4.2 %collective-permute-start.4 = (bf16[1,64,1,256]{3,2,1,0:T(2,128)(2,1)S(1)}, bf16[1,64,1,256]{3,2,1,0:T(2,128)(2,1)S(1)}, u32[]{:S(2)}, u32[]{:S(2)}) collective-permute-start(bf16[1,64,1,256]{3,2,1,0:T(2,128)(2,1)S(1)} %get-tuple-element.115), channel_id=1, source_target_pairs={{0,1},{1,2},{2,3},{4,5},{5,6},{6,7},{8,9},{9,10},{10,11},{12,13},{... | collective-permute-start | bytes 98312 | tf_op jit(solution)/shard_map/ppermute | solution.py:18
  46.1 2.5 %collective-permute-done.5 = bf16[1,64,1,256]{3,2,1,0:T(2,128)(2,1)S(1)} collective-permute-done((bf16[1,64,1,256]{3,2,1,0:T(2,128)(2,1)S(1)}, bf16[1,64,1,256]{3,2,1,0:T(2,128)(2,1)S(1)}, u32[]{:S(2)}, u32[]{:S(2)}) %collective-permute-start.5) | collective-permute-done | bytes 32800 | tf_op jit(solution)/shard_map/ppermute | solution.py:19
  60.3 2.1 copy.253
  62.5 2.1 multiply_reduce_fusion.2
  66.5 4.8 %collective-permute-start.14 = (bf16[1,64,1,128]{1,3,2,0:T(8,128)(2,1)S(1)}, bf16[1,64,1,128]{1,3,2,0:T(8,128)(2,1)S(1)}, u32[]{:S(2)}, u32[]{:S(2)}) collective-permute-start(bf16[1,64,1,128]{1,3,2,0:T(8,128)(2,1)S(1)} %get-tuple-element.175), channel_id=1, source_target_pairs={{0,1},{1,2},{2,3},{4,5},{5,6},{6,7},{8,9},{9,10},{10,11},{12,13},{... | collective-permute-start | bytes 49160 | tf_op jit(solution)/shard_map/ppermute | solution.py:18
  72.8 3.0 %collective-permute-start.10 = (bf16[1,64,1,128]{1,3,2,0:T(8,128)(2,1)S(1)}, bf16[1,64,1,128]{1,3,2,0:T(8,128)(2,1)S(1)}, u32[]{:S(2)}, u32[]{:S(2)}) collective-permute-start(bf16[1,64,1,128]{1,3,2,0:T(8,128)(2,1)S(1)} %get-tuple-element.167), channel_id=1, source_target_pairs={{0,1},{1,2},{2,3},{4,5},{5,6},{6,7},{8,9},{9,10},{10,11},{12,13},{... | collective-permute-start | bytes 49160 | tf_op jit(solution)/shard_map/ppermute | solution.py:18
  77.8 2.0 collective-permute-done.11
  83.6 4.5 %collective-permute-start.16 = (bf16[1,128,1,128]{1,3,2,0:T(8,128)(2,1)S(1)}, bf16[1,128,1,128]{1,3,2,0:T(8,128)(2,1)S(1)}, u32[]{:S(2)}, u32[]{:S(2)}) collective-permute-start(bf16[1,128,1,128]{1,3,2,0:T(8,128)(2,1)S(1)} %get-tuple-element.171), channel_id=1, source_target_pairs={{0,1},{1,2},{2,3},{4,5},{5,6},{6,7},{8,9},{9,10},{10,11},{12,13},{... | collective-permute-start | bytes 98312 | tf_op jit(solution)/shard_map/ppermute | solution.py:18
  89.5 3.0 %collective-permute-start.12 = (bf16[1,128,1,128]{1,3,2,0:T(8,128)(2,1)S(1)}, bf16[1,128,1,128]{1,3,2,0:T(8,128)(2,1)S(1)}, u32[]{:S(2)}, u32[]{:S(2)}) collective-permute-start(bf16[1,128,1,128]{1,3,2,0:T(8,128)(2,1)S(1)} %get-tuple-element.163), channel_id=1, source_target_pairs={{0,1},{1,2},{2,3},{4,5},{5,6},{6,7},{8,9},{9,10},{10,11},{12,13},{... | collective-permute-start | bytes 98312 | tf_op jit(solution)/shard_map/ppermute | solution.py:18
  100.4 4.7 %collective-permute-start.18 = (bf16[1,128,1,128]{1,3,2,0:T(8,128)(2,1)S(1)}, bf16[1,128,1,128]{1,3,2,0:T(8,128)(2,1)S(1)}, u32[]{:S(2)}, u32[]{:S(2)}) collective-permute-start(bf16[1,128,1,128]{1,3,2,0:T(8,128)(2,1)S(1)} %get-tuple-element.159), channel_id=1, source_target_pairs={{0,1},{1,2},{2,3},{4,5},{5,6},{6,7},{8,9},{9,10},{10,11},{12,13},{... | collective-permute-start | bytes 98312 | tf_op jit(solution)/shard_map/ppermute | solution.py:18
  106.4 1.8 collective-permute-done.19
  110.5 4.0 %collective-permute-start.20 = (bf16[1,128,1,128]{1,3,2,0:T(8,128)(2,1)S(1)}, bf16[1,128,1,128]{1,3,2,0:T(8,128)(2,1)S(1)}, u32[]{:S(2)}, u32[]{:S(2)}) collective-permute-start(bf16[1,128,1,128]{1,3,2,0:T(8,128)(2,1)S(1)} %get-tuple-element.155), channel_id=1, source_target_pairs={{0,1},{1,2},{2,3},{4,5},{5,6},{6,7},{8,9},{9,10},{10,11},{12,13},{... | collective-permute-start | bytes 98312 | tf_op jit(solution)/shard_map/ppermute | solution.py:18
  116.1 1.7 multiply_reduce_fusion
  124.1 2.0 fusion.35
  126.8 3.7 %collective-permute-start.22 = (bf16[1,64,1,256]{3,2,1,0:T(2,128)(2,1)}, bf16[1,64,1,256]{3,2,1,0:T(2,128)(2,1)}, u32[]{:S(2)}, u32[]{:S(2)}) collective-permute-start(bf16[1,64,1,256]{3,2,1,0:T(2,128)(2,1)} %get-tuple-element.107), channel_id=1, source_target_pairs={{0,1},{1,2},{2,3},{4,5},{5,6},{6,7},{8,9},{9,10},{10,11},{12,13},{... | collective-permute-start | bytes 98312 | tf_op jit(solution)/shard_map/ppermute | solution.py:18
  141.2 3.3 %collective-permute-start.24 = (bf16[1,64,1,256]{3,2,1,0:T(2,128)(2,1)S(1)}, bf16[1,64,1,256]{3,2,1,0:T(2,128)(2,1)S(1)}, u32[]{:S(2)}, u32[]{:S(2)}) collective-permute-start(bf16[1,64,1,256]{3,2,1,0:T(2,128)(2,1)S(1)} %get-tuple-element.103), channel_id=1, source_target_pairs={{0,1},{1,2},{2,3},{4,5},{5,6},{6,7},{8,9},{9,10},{10,11},{12,13},{... | collective-permute-start | bytes 98312 | tf_op jit(solution)/shard_map/ppermute | solution.py:18
  146.0 2.8 %collective-permute-done.25 = bf16[1,64,1,256]{3,2,1,0:T(2,128)(2,1)S(1)} collective-permute-done((bf16[1,64,1,256]{3,2,1,0:T(2,128)(2,1)S(1)}, bf16[1,64,1,256]{3,2,1,0:T(2,128)(2,1)S(1)}, u32[]{:S(2)}, u32[]{:S(2)}) %collective-permute-start.25) | collective-permute-done | bytes 32800 | tf_op jit(solution)/shard_map/ppermute | solution.py:19
  151.6 4.8 %collective-permute-start.26 = (bf16[1,3,1,256]{3,1,2,0:T(4,128)(2,1)S(1)}, bf16[1,3,1,256]{3,1,2,0:T(4,128)(2,1)S(1)}, u32[]{:S(2)}, u32[]{:S(2)}) collective-permute-start(bf16[1,3,1,256]{3,1,2,0:T(4,128)(2,1)S(1)} %get-tuple-element.197), channel_id=1, source_target_pairs={{0,1},{1,2},{2,3},{4,5},{5,6},{6,7},{8,9},{9,10},{10,11},{12,13},{... | collective-permute-start | bytes 4616 | tf_op jit(solution)/shard_map/ppermute | solution.py:18
  166.8 37.9 %all-reduce.17 = (f32[]{:T(128)}, f32[3,128,3,3]{1,3,2,0:T(4,128)S(1)}, f32[3]{0:T(128)S(1)}) all-reduce(f32[]{:T(128)S(6)} %add.1142, f32[3,128,3,3]{1,3,2,0:T(4,128)S(1)} %bitcast.1222, f32[3]{0:T(128)S(1)} %get-tuple-element.60), channel_id=1, replica_groups=mesh['clip'=8,'row'=4] {'clip'}, use_global_device_ids=true, to_apply=%region_8.9 | all-reduce | flops 3460 | bytes 27680 | tf_op jit(solution)/shard_map/psum | solution.py:211
  204.7 11.3 %all-reduce.18 = (f32[]{:T(128)}, f32[3,128,3,3]{1,3,2,0:T(4,128)}, f32[3]{0:T(128)}) all-reduce(f32[]{:T(128)} %get-tuple-element.54, f32[3,128,3,3]{1,3,2,0:T(4,128)S(1)} %get-tuple-element.55, f32[3]{0:T(128)S(1)} %get-tuple-element.56), channel_id=1, replica_groups=mesh['clip'=8,'row'=4] {'row'}, use_global_device_ids=true, to_apply=%region_9.10 | all-reduce | flops 3460 | bytes 27680 | tf_op jit(solution)/shard_map/psum | solution.py:210
  (419 shorter events, 89.2 us)
Async XLA Ops:
  3.4 12.1 %collective-permute-start = (f32[1,3,256]{2,1,0:T(4,128)S(1)}, f32[1,3,256]{2,1,0:T(4,128)S(1)}, u32[]{:S(2)}, u32[]{:S(2)}) collective-permute-start(f32[1,3,256]{2,1,0:T(4,128)S(1)} %fusion.18), channel_id=1, source_target_pairs={{0,1},{1,2},{2,3},{4,5},{5,6},{6,7},{8,9},{9,10},{10,11},{12,13},{... | collective-permute-start | bytes 9224 | tf_op jit(solution)/shard_map/ppermute | solution.py:27
  6.4 9.2 %collective-permute-start.1 = (f32[1,3,256]{2,1,0:T(4,128)S(1)}, f32[1,3,256]{2,1,0:T(4,128)S(1)}, u32[]{:S(2)}, u32[]{:S(2)}) collective-permute-start(f32[1,3,256]{2,1,0:T(4,128)S(1)} %fusion.17), channel_id=1, source_target_pairs={{1,0},{2,1},{3,2},{5,4},{6,5},{7,6},{9,8},{10,9},{11,10},{13,12},{... | collective-permute-start | bytes 9224 | tf_op jit(solution)/shard_map/ppermute | solution.py:27
  15.7 12.1 %collective-permute-start.2 = (bf16[1,3,1,256]{3,1,2,0:T(4,128)(2,1)S(1)}, bf16[1,3,1,256]{3,1,2,0:T(4,128)(2,1)S(1)}, u32[]{:S(2)}, u32[]{:S(2)}) collective-permute-start(bf16[1,3,1,256]{3,1,2,0:T(4,128)(2,1)S(1)} %get-tuple-element.205), channel_id=1, source_target_pairs={{0,1},{1,2},{2,3},{4,5},{5,6},{6,7},{8,9},{9,10},{10,11},{12,13},{... | collective-permute-start | bytes 4616 | tf_op jit(solution)/shard_map/ppermute | solution.py:18
  20.9 6.9 %collective-permute-start.3 = (bf16[1,3,1,256]{3,1,2,0:T(4,128)(2,1)S(1)}, bf16[1,3,1,256]{3,1,2,0:T(4,128)(2,1)S(1)}, u32[]{:S(2)}, u32[]{:S(2)}) collective-permute-start(bf16[1,3,1,256]{3,1,2,0:T(4,128)(2,1)S(1)} %get-tuple-element.206), channel_id=1, source_target_pairs={{1,0},{2,1},{3,2},{5,4},{6,5},{7,6},{9,8},{10,9},{11,10},{13,12},{... | collective-permute-start | bytes 4616 | tf_op jit(solution)/shard_map/ppermute | solution.py:19
  22.2 8.5 %collective-permute-start.6 = (bf16[1,3,1,256]{3,1,2,0:T(4,128)(2,1)S(1)}, bf16[1,3,1,256]{3,1,2,0:T(4,128)(2,1)S(1)}, u32[]{:S(2)}, u32[]{:S(2)}) collective-permute-start(bf16[1,3,1,256]{3,1,2,0:T(4,128)(2,1)S(1)} %get-tuple-element.201), channel_id=1, source_target_pairs={{0,1},{1,2},{2,3},{4,5},{5,6},{6,7},{8,9},{9,10},{10,11},{12,13},{... | collective-permute-start | bytes 4616 | tf_op jit(solution)/shard_map/ppermute | solution.py:18
  26.5 4.3 %collective-permute-start.7 = (bf16[1,3,1,256]{3,1,2,0:T(4,128)(2,1)S(1)}, bf16[1,3,1,256]{3,1,2,0:T(4,128)(2,1)S(1)}, u32[]{:S(2)}, u32[]{:S(2)}) collective-permute-start(bf16[1,3,1,256]{3,1,2,0:T(4,128)(2,1)S(1)} %get-tuple-element.202), channel_id=1, source_target_pairs={{1,0},{2,1},{3,2},{5,4},{6,5},{7,6},{9,8},{10,9},{11,10},{13,12},{... | collective-permute-start | bytes 4616 | tf_op jit(solution)/shard_map/ppermute | solution.py:19
  34.2 11.5 %collective-permute-start.8 = (bf16[1,64,1,256]{3,2,1,0:T(2,128)(2,1)S(1)}, bf16[1,64,1,256]{3,2,1,0:T(2,128)(2,1)S(1)}, u32[]{:S(2)}, u32[]{:S(2)}) collective-permute-start(bf16[1,64,1,256]{3,2,1,0:T(2,128)(2,1)S(1)} %get-tuple-element.111), channel_id=1, source_target_pairs={{0,1},{1,2},{2,3},{4,5},{5,6},{6,7},{8,9},{9,10},{10,11},{12,13},{... | collective-permute-start | bytes 98312 | tf_op jit(solution)/shard_map/ppermute | solution.py:18
  38.5 7.2 %collective-permute-start.9 = (bf16[1,64,1,256]{3,2,1,0:T(2,128)(2,1)S(1)}, bf16[1,64,1,256]{3,2,1,0:T(2,128)(2,1)S(1)}, u32[]{:S(2)}, u32[]{:S(2)}) collective-permute-start(bf16[1,64,1,256]{3,2,1,0:T(2,128)(2,1)S(1)} %get-tuple-element.112), channel_id=1, source_target_pairs={{1,0},{2,1},{3,2},{5,4},{6,5},{7,6},{9,8},{10,9},{11,10},{13,12},{... | collective-permute-start | bytes 98312 | tf_op jit(solution)/shard_map/ppermute | solution.py:19
  40.0 6.1 %collective-permute-start.4 = (bf16[1,64,1,256]{3,2,1,0:T(2,128)(2,1)S(1)}, bf16[1,64,1,256]{3,2,1,0:T(2,128)(2,1)S(1)}, u32[]{:S(2)}, u32[]{:S(2)}) collective-permute-start(bf16[1,64,1,256]{3,2,1,0:T(2,128)(2,1)S(1)} %get-tuple-element.115), channel_id=1, source_target_pairs={{0,1},{1,2},{2,3},{4,5},{5,6},{6,7},{8,9},{9,10},{10,11},{12,13},{... | collective-permute-start | bytes 98312 | tf_op jit(solution)/shard_map/ppermute | solution.py:18
  44.2 4.4 %collective-permute-start.5 = (bf16[1,64,1,256]{3,2,1,0:T(2,128)(2,1)S(1)}, bf16[1,64,1,256]{3,2,1,0:T(2,128)(2,1)S(1)}, u32[]{:S(2)}, u32[]{:S(2)}) collective-permute-start(bf16[1,64,1,256]{3,2,1,0:T(2,128)(2,1)S(1)} %get-tuple-element.116), channel_id=1, source_target_pairs={{1,0},{2,1},{3,2},{5,4},{6,5},{7,6},{9,8},{10,9},{11,10},{13,12},{... | collective-permute-start | bytes 98312 | tf_op jit(solution)/shard_map/ppermute | solution.py:19
  66.5 10.7 %collective-permute-start.14 = (bf16[1,64,1,128]{1,3,2,0:T(8,128)(2,1)S(1)}, bf16[1,64,1,128]{1,3,2,0:T(8,128)(2,1)S(1)}, u32[]{:S(2)}, u32[]{:S(2)}) collective-permute-start(bf16[1,64,1,128]{1,3,2,0:T(8,128)(2,1)S(1)} %get-tuple-element.175), channel_id=1, source_target_pairs={{0,1},{1,2},{2,3},{4,5},{5,6},{6,7},{8,9},{9,10},{10,11},{12,13},{... | collective-permute-start | bytes 49160 | tf_op jit(solution)/shard_map/ppermute | solution.py:18
  71.4 5.8 %collective-permute-start.15 = (bf16[1,64,1,128]{1,3,2,0:T(8,128)(2,1)S(1)}, bf16[1,64,1,128]{1,3,2,0:T(8,128)(2,1)S(1)}, u32[]{:S(2)}, u32[]{:S(2)}) collective-permute-start(bf16[1,64,1,128]{1,3,2,0:T(8,128)(2,1)S(1)} %get-tuple-element.176), channel_id=1, source_target_pairs={{1,0},{2,1},{3,2},{5,4},{6,5},{7,6},{9,8},{10,9},{11,10},{13,12},{... | collective-permute-start | bytes 49160 | tf_op jit(solution)/shard_map/ppermute | solution.py:19
  72.8 4.9 %collective-permute-start.10 = (bf16[1,64,1,128]{1,3,2,0:T(8,128)(2,1)S(1)}, bf16[1,64,1,128]{1,3,2,0:T(8,128)(2,1)S(1)}, u32[]{:S(2)}, u32[]{:S(2)}) collective-permute-start(bf16[1,64,1,128]{1,3,2,0:T(8,128)(2,1)S(1)} %get-tuple-element.167), channel_id=1, source_target_pairs={{0,1},{1,2},{2,3},{4,5},{5,6},{6,7},{8,9},{9,10},{10,11},{12,13},{... | collective-permute-start | bytes 49160 | tf_op jit(solution)/shard_map/ppermute | solution.py:18
  83.6 10.2 %collective-permute-start.16 = (bf16[1,128,1,128]{1,3,2,0:T(8,128)(2,1)S(1)}, bf16[1,128,1,128]{1,3,2,0:T(8,128)(2,1)S(1)}, u32[]{:S(2)}, u32[]{:S(2)}) collective-permute-start(bf16[1,128,1,128]{1,3,2,0:T(8,128)(2,1)S(1)} %get-tuple-element.171), channel_id=1, source_target_pairs={{0,1},{1,2},{2,3},{4,5},{5,6},{6,7},{8,9},{9,10},{10,11},{12,13},{... | collective-permute-start | bytes 98312 | tf_op jit(solution)/shard_map/ppermute | solution.py:18
  88.1 5.7 %collective-permute-start.17 = (bf16[1,128,1,128]{1,3,2,0:T(8,128)(2,1)S(1)}, bf16[1,128,1,128]{1,3,2,0:T(8,128)(2,1)S(1)}, u32[]{:S(2)}, u32[]{:S(2)}) collective-permute-start(bf16[1,128,1,128]{1,3,2,0:T(8,128)(2,1)S(1)} %get-tuple-element.172), channel_id=1, source_target_pairs={{1,0},{2,1},{3,2},{5,4},{6,5},{7,6},{9,8},{10,9},{11,10},{13,12},{... | collective-permute-start | bytes 98312 | tf_op jit(solution)/shard_map/ppermute | solution.py:19
  89.5 5.7 %collective-permute-start.12 = (bf16[1,128,1,128]{1,3,2,0:T(8,128)(2,1)S(1)}, bf16[1,128,1,128]{1,3,2,0:T(8,128)(2,1)S(1)}, u32[]{:S(2)}, u32[]{:S(2)}) collective-permute-start(bf16[1,128,1,128]{1,3,2,0:T(8,128)(2,1)S(1)} %get-tuple-element.163), channel_id=1, source_target_pairs={{0,1},{1,2},{2,3},{4,5},{5,6},{6,7},{8,9},{9,10},{10,11},{12,13},{... | collective-permute-start | bytes 98312 | tf_op jit(solution)/shard_map/ppermute | solution.py:18
  100.4 6.0 %collective-permute-start.18 = (bf16[1,128,1,128]{1,3,2,0:T(8,128)(2,1)S(1)}, bf16[1,128,1,128]{1,3,2,0:T(8,128)(2,1)S(1)}, u32[]{:S(2)}, u32[]{:S(2)}) collective-permute-start(bf16[1,128,1,128]{1,3,2,0:T(8,128)(2,1)S(1)} %get-tuple-element.159), channel_id=1, source_target_pairs={{0,1},{1,2},{2,3},{4,5},{5,6},{6,7},{8,9},{9,10},{10,11},{12,13},{... | collective-permute-start | bytes 98312 | tf_op jit(solution)/shard_map/ppermute | solution.py:18
  110.5 9.3 %collective-permute-start.20 = (bf16[1,128,1,128]{1,3,2,0:T(8,128)(2,1)S(1)}, bf16[1,128,1,128]{1,3,2,0:T(8,128)(2,1)S(1)}, u32[]{:S(2)}, u32[]{:S(2)}) collective-permute-start(bf16[1,128,1,128]{1,3,2,0:T(8,128)(2,1)S(1)} %get-tuple-element.155), channel_id=1, source_target_pairs={{0,1},{1,2},{2,3},{4,5},{5,6},{6,7},{8,9},{9,10},{10,11},{12,13},{... | collective-permute-start | bytes 98312 | tf_op jit(solution)/shard_map/ppermute | solution.py:18
  114.6 5.2 %collective-permute-start.21 = (bf16[1,128,1,128]{1,3,2,0:T(8,128)(2,1)S(1)}, bf16[1,128,1,128]{1,3,2,0:T(8,128)(2,1)S(1)}, u32[]{:S(2)}, u32[]{:S(2)}) collective-permute-start(bf16[1,128,1,128]{1,3,2,0:T(8,128)(2,1)S(1)} %get-tuple-element.156), channel_id=1, source_target_pairs={{1,0},{2,1},{3,2},{5,4},{6,5},{7,6},{9,8},{10,9},{11,10},{13,12},{... | collective-permute-start | bytes 98312 | tf_op jit(solution)/shard_map/ppermute | solution.py:19
  126.8 7.8 %collective-permute-start.22 = (bf16[1,64,1,256]{3,2,1,0:T(2,128)(2,1)}, bf16[1,64,1,256]{3,2,1,0:T(2,128)(2,1)}, u32[]{:S(2)}, u32[]{:S(2)}) collective-permute-start(bf16[1,64,1,256]{3,2,1,0:T(2,128)(2,1)} %get-tuple-element.107), channel_id=1, source_target_pairs={{0,1},{1,2},{2,3},{4,5},{5,6},{6,7},{8,9},{9,10},{10,11},{12,13},{... | collective-permute-start | bytes 98312 | tf_op jit(solution)/shard_map/ppermute | solution.py:18
  130.5 5.0 %collective-permute-start.23 = (bf16[1,64,1,256]{3,2,1,0:T(2,128)(2,1)}, bf16[1,64,1,256]{3,2,1,0:T(2,128)(2,1)S(1)}, u32[]{:S(2)}, u32[]{:S(2)}) collective-permute-start(bf16[1,64,1,256]{3,2,1,0:T(2,128)(2,1)} %get-tuple-element.108), channel_id=1, source_target_pairs={{1,0},{2,1},{3,2},{5,4},{6,5},{7,6},{9,8},{10,9},{11,10},{13,12},{... | collective-permute-start | bytes 98312 | tf_op jit(solution)/shard_map/ppermute | solution.py:19
  141.2 4.8 %collective-permute-start.24 = (bf16[1,64,1,256]{3,2,1,0:T(2,128)(2,1)S(1)}, bf16[1,64,1,256]{3,2,1,0:T(2,128)(2,1)S(1)}, u32[]{:S(2)}, u32[]{:S(2)}) collective-permute-start(bf16[1,64,1,256]{3,2,1,0:T(2,128)(2,1)S(1)} %get-tuple-element.103), channel_id=1, source_target_pairs={{0,1},{1,2},{2,3},{4,5},{5,6},{6,7},{8,9},{9,10},{10,11},{12,13},{... | collective-permute-start | bytes 98312 | tf_op jit(solution)/shard_map/ppermute | solution.py:18
  144.6 4.2 %collective-permute-start.25 = (bf16[1,64,1,256]{3,2,1,0:T(2,128)(2,1)S(1)}, bf16[1,64,1,256]{3,2,1,0:T(2,128)(2,1)S(1)}, u32[]{:S(2)}, u32[]{:S(2)}) collective-permute-start(bf16[1,64,1,256]{3,2,1,0:T(2,128)(2,1)S(1)} %get-tuple-element.104), channel_id=1, source_target_pairs={{1,0},{2,1},{3,2},{5,4},{6,5},{7,6},{9,8},{10,9},{11,10},{13,12},{... | collective-permute-start | bytes 98312 | tf_op jit(solution)/shard_map/ppermute | solution.py:19
  151.6 7.8 %collective-permute-start.26 = (bf16[1,3,1,256]{3,1,2,0:T(4,128)(2,1)S(1)}, bf16[1,3,1,256]{3,1,2,0:T(4,128)(2,1)S(1)}, u32[]{:S(2)}, u32[]{:S(2)}) collective-permute-start(bf16[1,3,1,256]{3,1,2,0:T(4,128)(2,1)S(1)} %get-tuple-element.197), channel_id=1, source_target_pairs={{0,1},{1,2},{2,3},{4,5},{5,6},{6,7},{8,9},{9,10},{10,11},{12,13},{... | collective-permute-start | bytes 4616 | tf_op jit(solution)/shard_map/ppermute | solution.py:18
  (43 other events, 118.7 us)
